TPU v7x, 32 devices: a whole 2x2x4 slice. The times are simulated.
32 devices in a mesh: vessel: 2 (over core), gather: 16 (over z, y, x).
Axes of the slice: x: 2, y: 2, z: 4, core: 2. Of those that a mesh axis runs over, the one named last changes fastest.
Arguments:
- observed: bfloat16 [16, 16, 2048], P('gather'), may hold values from -6 to 6
- estimate: bfloat16 [2, 16, 16, 2048], P('vessel', 'gather'), may hold values from -6 to 6
- delays: int32 [2, 16], P('vessel', 'gather'), may hold values from 0 to 256
- taps_time: float32 [16, 7], replicated, may hold values from -2 to 2
- taps_shot: float32 [16, 7], replicated, may hold values from -0.5 to 0.5
- thresh: float32 [16], replicated, may hold values from 0.02 to 0.3
Outputs:
- deblended: bfloat16 [2, 16, 16, 2048], P('vessel', 'gather')
All inputs are finite; a program needn't handle non-finite values.
Results may differ from a plain program's by a relative error of at most 0.022.
Values may be sent and summed in bfloat16 or wider, within the bound.
A program may use at most 64 MiB of HBM per device.

v0:
```python
import functools

import jax
import jax.numpy as jnp
from jax import lax
from jax.experimental import pallas as pl
from jax.experimental.pallas import tpu as pltpu
from jax.sharding import PartitionSpec as P

TIME_SPACING = 4
SHOT_SPACING = 2
MAXD = 256
ITERS = 2
LANES = 128
REACH = 3

MESH = pl.DeviceIdType.MESH


def partner_of(me, i, n):
    return me ^ (n - i) if n & (n - 1) == 0 else lax.rem(me + i, n)


def across(column, extent):
    return jnp.concatenate([column] * (extent // LANES), axis=1)


def shift_left(padded, amount, width, top):
    def choose(step, moved, kept):
        bit = ((amount & step) != 0).astype(jnp.float32)
        extent = moved.shape[1]
        taken = across(bit.astype(jnp.bfloat16), extent)
        left = across((1.0 - bit).astype(jnp.bfloat16), extent)
        return moved * taken + kept * left

    current = padded
    step = top
    keep = top
    while step >= LANES:
        current = choose(step, current[:, step : step + width + keep], current[:, : width + keep])
        step //= 2
        keep = step
    extent = width + LANES
    current = current[:, :extent]
    while step >= 1:
        current = choose(step, pltpu.roll(current, extent - step, 1), current)
        step //= 2
    return current[:, :width]


def kernel(
    dims,
    x_hbm,
    obs_hbm,
    d_hbm,
    tt_hbm,
    ts_hbm,
    th_hbm,
    out_ref,
    x_ref,
    obs_ref,
    d_ref,
    tt_ref,
    ts_ref,
    th_ref,
    s_in,
    flat,
    flat2,
    stage,
    rbuf,
    dsend,
    drecv,
    m_s,
    mt_s,
    th_s,
    pst,
    g_s,
    tail_s,
    tail_r,
    stage2,
    rbuf2,
    s_pay,
    r_pay,
    s_del,
    r_del,
    s_tail,
    r_tail,
    s_out,
    r_out,
):
    n, width, channels, taps, chunks, rows, depth = dims
    v = lax.axis_index("vessel")
    me = lax.axis_index("gather")
    other = 1 - v
    nt = width // LANES
    group = rows // n

    barrier = pltpu.get_barrier_semaphore()

    def greet(i, carry):
        p = lax.rem(me + i, n)
        pl.semaphore_signal(barrier, inc=1, device_id=(v, p), device_id_type=MESH)
        pl.semaphore_signal(barrier, inc=1, device_id=(other, p), device_id_type=MESH)
        return carry

    lax.fori_loop(1, n, greet, 0)
    pl.semaphore_signal(barrier, inc=1, device_id=(other, me), device_id_type=MESH)

    loads = [
        pltpu.make_async_copy(source, target, s_in.at[i])
        for i, (source, target) in enumerate(
            (
                (x_hbm, x_ref),
                (obs_hbm, obs_ref),
                (d_hbm, d_ref),
                (tt_hbm, tt_ref),
                (ts_hbm, ts_ref),
                (th_hbm, th_ref),
            )
        )
    ]
    for load in loads:
        load.start()
    for load in loads[:3]:
        load.wait()

    def to_rows(ref, value):
        for i in range(nt):
            ref[pl.ds(i, n, stride=nt), :] = value[:, i * LANES : (i + 1) * LANES]

    def from_rows(ref):
        return jnp.concatenate([ref[pl.ds(i, n, stride=nt), :] for i in range(nt)], axis=1)

    to_rows(flat, x_ref[0, 0].astype(jnp.float32))
    to_rows(flat2, obs_ref[0].astype(jnp.float32))
    stage[:, 0] = flat[...].reshape(n, nt, LANES).astype(jnp.bfloat16)
    stage[:, 1] = flat2[...].reshape(n, nt, LANES).astype(jnp.bfloat16)
    dsend[...] = jnp.broadcast_to(d_ref[...], (1, LANES))

    pl.semaphore_wait(barrier, 2 * n - 1)

    def payload(p, send_at, recv_at, slot):
        return pltpu.make_async_remote_copy(
            src_ref=stage.at[p],
            dst_ref=rbuf.at[slot],
            send_sem=s_pay.at[send_at],
            recv_sem=r_pay.at[recv_at],
            device_id=(v, p),
            device_id_type=MESH,
        )

    def delay(to_vessel, p, side, send_at, vessel_at, shot_at):
        return pltpu.make_async_remote_copy(
            src_ref=dsend,
            dst_ref=drecv.at[vessel_at, shot_at],
            send_sem=s_del.at[side, send_at],
            recv_sem=r_del.at[vessel_at, shot_at],
            device_id=(to_vessel, p),
            device_id_type=MESH,
        )

    def send(i, carry):
        p = partner_of(me, i, n)
        payload(p, i, me, me).start()
        return carry

    def send_delay(i, carry):
        p = partner_of(me, i, n)
        delay(v, p, 0, i, v, me).start()
        delay(other, p, 1, i, v, me).start()
        return carry

    lax.fori_loop(1, n, send, 0)
    lax.fori_loop(1, n, send_delay, 0)
    delay(other, me, 1, 0, v, me).start()
    rbuf[me] = stage[me]
    drecv[v, me] = dsend[...]

    for load in loads[3:]:
        load.wait()

    def build(q, carry):
        row_ch = q * group + lax.broadcasted_iota(jnp.int32, (rows, channels), 0) // n
        pick = row_ch == lax.broadcasted_iota(jnp.int32, (rows, channels), 1)
        pick_f = pick.astype(jnp.float32)
        tt = lax.dot_general(pick_f, tt_ref[...], (((1,), (1,)), ((), ())), precision=lax.Precision.HIGHEST, preferred_element_type=jnp.float32)
        ts = lax.dot_general(pick_f, ts_ref[...], (((1,), (1,)), ((), ())), precision=lax.Precision.HIGHEST, preferred_element_type=jnp.float32)
        th_s[q] = jnp.broadcast_to(jnp.sum(jnp.where(pick, th_ref[...], 0.0), axis=1, keepdims=True), (rows, LANES))
        col = lax.broadcasted_iota(jnp.int32, (rows, depth), 1)
        row = lax.broadcasted_iota(jnp.int32, (rows, depth), 0)
        apart = lax.rem(col, n) - lax.rem(row, n)
        tap_of = col // n
        a = jnp.zeros((rows, depth), jnp.float32)
        b = jnp.zeros((rows, depth), jnp.float32)
        for k in range(taps):
            a = jnp.where(tap_of == k, tt[:, k : k + 1], a)
            b = jnp.where(apart == (k - REACH) * SHOT_SPACING, ts[:, k : k + 1], b)
        m = a * b
        m_s[q] = m.astype(jnp.bfloat16)
        mt_s[q] = m.T.astype(jnp.bfloat16)
        return carry

    if chunks == 1:
        build(0, 0)
    else:
        lax.fori_loop(0, chunks, build, 0)
    if depth > taps * n:
        pst[taps * n :, :] = jnp.zeros((depth - taps * n, width), jnp.bfloat16)

    def arrive(i, carry):
        p = partner_of(me, i, n)
        payload(p, i, p, p).wait_recv()
        delay(v, p, 0, i, v, p).wait_recv()
        delay(v, p, 0, i, other, p).wait_recv()
        return carry

    delay(other, me, 1, 0, other, me).wait_recv()
    lax.fori_loop(1, n, arrive, 0)

    flat[...] = rbuf[:, 0].astype(jnp.float32).reshape(n * nt, LANES)
    flat2[...] = rbuf[:, 1].astype(jnp.float32).reshape(n * nt, LANES)
    held = from_rows(flat).astype(jnp.bfloat16)
    observed = from_rows(flat2).astype(jnp.bfloat16)
    d_mine = drecv[v].reshape(n, LANES)
    d_other = drecv[other].reshape(n, LANES)

    early_mark = width - 2 * MAXD
    block_width = 2048

    def filter_columns(start, stop):
        def one(q, first):
            for c0 in range(start, stop, block_width):
                c1 = min(c0 + block_width, stop)
                y = jnp.dot(m_s[q], pst[:, c0:c1], preferred_element_type=jnp.float32)
                th = across(th_s[q], c1 - c0)
                z = (y - jnp.minimum(jnp.maximum(y, -th), th)).astype(jnp.bfloat16)
                g = jnp.dot(mt_s[q], z, preferred_element_type=jnp.float32)
                if first:
                    g_s[:, c0:c1] = g
                else:
                    g_s[:, c0:c1] += g

        one(0, True)
        if chunks > 1:

            def more(q, carry):
                one(q, False)
                return carry

            lax.fori_loop(1, chunks, more, 0)

    def stack_taps(piece, lead, start, stop):
        extent = piece.shape[1]
        for k in range(taps):
            step = (k - REACH) * TIME_SPACING
            moved = piece if step == 0 else pltpu.roll(piece, (extent - step) % extent, 1)
            pst[k * n : (k + 1) * n, start:stop] = moved[:, lead : lead + stop - start]

    zeros = lambda w, t=jnp.bfloat16: jnp.zeros((n, w), t)

    def tail_copy(it):
        return pltpu.make_async_remote_copy(
            src_ref=tail_s.at[it],
            dst_ref=tail_r.at[it],
            send_sem=s_tail.at[it],
            recv_sem=r_tail.at[it],
            device_id=(other, me),
            device_id_type=MESH,
        )

    for it in range(ITERS):
        d_held, d_plane = (d_mine, d_other) if it % 2 == 0 else (d_other, d_mine)
        tail_s[it] = held[:, width - MAXD :]
        tail_copy(it).start()
        seen = shift_left(jnp.concatenate([observed, zeros(2 * MAXD)], axis=1), d_plane, width, MAXD)
        crossed = shift_left(
            jnp.concatenate([zeros(MAXD), held, zeros(3 * MAXD)], axis=1),
            d_plane - d_held + MAXD,
            width,
            2 * MAXD,
        )
        exact = seen.astype(jnp.float32) - crossed.astype(jnp.float32)
        plane = exact.astype(jnp.bfloat16)
        stack_taps(
            jnp.concatenate([plane[:, : early_mark + LANES], zeros(LANES)], axis=1), 0, 0, early_mark
        )
        filter_columns(0, early_mark)
        tail_copy(it).wait_recv()
        cut = width - MAXD
        time = cut + lax.broadcasted_iota(jnp.int32, (n, MAXD), 1)
        end = jnp.where(time + across(d_plane, MAXD) < width, exact[:, cut:], tail_r[it].astype(jnp.float32))
        end = end.astype(jnp.bfloat16)
        stack_taps(
            jnp.concatenate([plane[:, early_mark - LANES : cut], end, zeros(LANES)], axis=1),
            LANES,
            early_mark,
            width,
        )
        filter_columns(early_mark, width)
        total = zeros(width, jnp.float32)
        for k in range(taps):
            step = (k - REACH) * TIME_SPACING
            g = g_s[k * n : (k + 1) * n, :]
            if step != 0:
                extent = width + LANES
                g = pltpu.roll(jnp.concatenate([g, zeros(LANES, jnp.float32)], axis=1), step % extent, 1)[:, :width]
            total = total + g
        held = total.astype(jnp.bfloat16)

    to_rows(flat, held.astype(jnp.float32))
    stage2[...] = flat[...].reshape(n, nt, LANES).astype(jnp.bfloat16)

    def result(p, send_at, recv_at, slot):
        return pltpu.make_async_remote_copy(
            src_ref=stage2.at[p],
            dst_ref=rbuf2.at[slot],
            send_sem=s_out.at[send_at],
            recv_sem=r_out.at[recv_at],
            device_id=(v, p),
            device_id_type=MESH,
        )

    def send_back(i, carry):
        p = partner_of(me, i, n)
        result(p, i, me, me).start()
        return carry

    lax.fori_loop(1, n, send_back, 0)
    rbuf2[me] = stage2[me]

    def sent(i, carry):
        p = partner_of(me, i, n)
        payload(p, i, p, p).wait_send()
        delay(v, p, 0, i, v, p).wait_send()
        delay(other, p, 1, i, v, p).wait_send()
        return carry

    delay(other, me, 1, 0, v, me).wait_send()
    lax.fori_loop(1, n, sent, 0)
    for it in range(ITERS):
        tail_copy(it).wait_send()

    def back(i, carry):
        p = partner_of(me, i, n)
        result(p, i, p, p).wait_recv()
        result(p, i, p, p).wait_send()
        return carry

    lax.fori_loop(1, n, back, 0)
    flat[...] = rbuf2[...].astype(jnp.float32).reshape(n * nt, LANES)
    out_ref[0, 0] = from_rows(flat).astype(jnp.bfloat16)


def per_device(n, observed, estimate, delays, taps_time, taps_shot, thresh):
    receivers, width = observed.shape[1:]
    channels, taps = taps_time.shape
    assert observed.shape[0] == 1 and receivers == n and width % LANES == 0
    group = max(1, min(channels, 256 // n))
    chunks = channels // group
    rows = group * n
    depth = -(-taps * n // LANES) * LANES
    nt = width // LANES
    bf16, f32 = jnp.bfloat16, jnp.float32
    vmem = pl.BlockSpec(memory_space=pltpu.VMEM)
    dma = pltpu.SemaphoreType.DMA
    operands = (estimate, observed, delays, taps_time.T, taps_shot.T, thresh.reshape(1, channels))
    operands = [
        operand if operand is delays else pltpu.with_memory_space_constraint(operand, pltpu.HBM)
        for operand in operands
    ]
    return pl.pallas_call(
        functools.partial(kernel, (n, width, channels, taps, chunks, rows, depth)),
        out_shape=pltpu.VMEM(estimate.shape, bf16),
        in_specs=[pl.BlockSpec(memory_space=pl.ANY)] * 6,
        out_specs=vmem,
        scratch_shapes=[
            pltpu.VMEM((1, 1, n, width), bf16),
            pltpu.VMEM((1, n, width), bf16),
            pltpu.VMEM((1, 1), jnp.int32),
            pltpu.VMEM((taps, channels), f32),
            pltpu.VMEM((taps, channels), f32),
            pltpu.VMEM((1, channels), f32),
            dma((6,)),
            pltpu.VMEM((n * nt, LANES), f32),
            pltpu.VMEM((n * nt, LANES), f32),
            pltpu.VMEM((n, 2, nt, LANES), bf16),
            pltpu.VMEM((n, 2, nt, LANES), bf16),
            pltpu.VMEM((1, LANES), jnp.int32),
            pltpu.VMEM((2, n, 1, LANES), jnp.int32),
            pltpu.VMEM((chunks, rows, depth), bf16),
            pltpu.VMEM((chunks, depth, rows), bf16),
            pltpu.VMEM((chunks, rows, LANES), f32),
            pltpu.VMEM((depth, width), bf16),
            pltpu.VMEM((depth, width), f32),
            pltpu.VMEM((ITERS, n, MAXD), bf16),
            pltpu.VMEM((ITERS, n, MAXD), bf16),
            pltpu.VMEM((n, nt, LANES), bf16),
            pltpu.VMEM((n, nt, LANES), bf16),
            dma((n,)),
            dma((n,)),
            dma((2, n)),
            dma((2, n)),
            dma((ITERS,)),
            dma((ITERS,)),
            dma((n,)),
            dma((n,)),
        ],
        compiler_params=pltpu.CompilerParams(collective_id=0, has_side_effects=True, vmem_limit_bytes=48 << 20),
        )(*operands)


def solution(mesh):
    return jax.shard_map(
        functools.partial(per_device, mesh.shape["gather"]),
        mesh=mesh,
        in_specs=(
            P("gather", None, None),
            P("vessel", "gather", None, None),
            P("vessel", "gather"),
            P(),
            P(),
            P(),
        ),
        out_specs=P("vessel", "gather", None, None),
        check_vma=False,
    )
```

profile of v0, /device:TPU:0, one launch (start us, length us, event | category | flops | bytes accessed | tf_op | source)
XLA Modules:
  0.0 24.4 jit_solution(12503158119988503366)
XLA Ops:
  0.7 23.1 %shard_map.64 = bf16[1,1,16,2048]{3,2,1,0:T(8,128)(2,1)S(1)} custom-call(bf16[1,1,16,2048]{3,2,1,0:T(8,128)(2,1)} %x_hbm.1, bf16[1,16,2048]{2,1,0:T(8,128)(2,1)} %obs_hbm.1, s32[1,1]{1,0:T(1,128)S(6)} %copy.9.d_hbm, f32[7,16]{1,0:T(8,128)} %bitcast.3, f32[7,16]{1,0:T(8,128)} %bitcast.4, f32[1,16]{1,0:T(1,128)} %bitcast.5), custom_call_target="tpu_custom_call" | custom-call | tf_op jit(solution)/shard_map/pallas_call | solution.py:371
  23.7 0.6 %copy.8 = bf16[1,1,16,2048]{3,2,1,0:T(8,128)(2,1)} copy(bf16[1,1,16,2048]{3,2,1,0:T(8,128)(2,1)S(1)} %shard_map.64) | data formatting | bytes 131072
where the time goes:
time: 24.5 us; the launch traced here: 24.4 us
  Pallas kernels  23.1 us (94%)
  between operations  0.66 us (3%)
  local copies, waits for them, and re-layouts  0.63 us (3%)
    pallas_call x1, Pallas kernels, per_device(): pl.pallas_call(functools.partial(kernel, (n, width, channels, taps, chunk...  23.1 us
    unnamed x1, local copies, waits for them, and re-layouts  0.63 us

commit v1 on v0

v1 whole, which is shorter than its diff:
```python
import functools

import jax
import jax.numpy as jnp
from jax import lax
from jax.experimental import pallas as pl
from jax.experimental.pallas import tpu as pltpu
from jax.sharding import PartitionSpec as P

TIME_SPACING = 4
SHOT_SPACING = 2
MAXD = 256
ITERS = 2
LANES = 128
REACH = 3
SIDE = 8

MESH = pl.DeviceIdType.MESH


def partner_of(me, i, n):
    return me ^ (n - i) if n & (n - 1) == 0 else lax.rem(me + i, n)


def across(column, extent):
    return jnp.concatenate([column] * (extent // LANES), axis=1)


def lane_of(shape):
    return lax.broadcasted_iota(jnp.int32, shape, 1)


def shift_rows(tiles, amount, count, most):
    shape = amount.shape
    zero = jnp.zeros(shape, jnp.float32)
    within = amount & (LANES - 1)
    whole = amount >> (LANES.bit_length() - 1)
    reach = lane_of(shape) + within
    index = reach & (LANES - 1)
    wrapped = reach >= LANES
    extent = count + most + 1
    tiles = list(tiles) + [None] * (extent - len(tiles))
    turned = [None if t is None else jnp.take_along_axis(t, index, axis=1, mode="promise_in_bounds") for t in tiles]

    def pick(mask, a, b):
        if a is None and b is None:
            return None
        return jnp.where(mask, zero if a is None else a, zero if b is None else b)

    level = [pick(wrapped, turned[j + 1], turned[j]) for j in range(extent - 1)]
    step = 1
    while step <= most:
        mask = (whole & step) != 0
        level = [
            pick(mask, level[j + step] if j + step < len(level) else None, level[j]) for j in range(len(level))
        ]
        step *= 2
    return [zero if t is None else t for t in level[:count]]


def kernel(
    dims,
    x_hbm,
    obs_hbm,
    d_hbm,
    tt_hbm,
    ts_hbm,
    th_hbm,
    out_ref,
    x_ref,
    obs_ref,
    tt_ref,
    ts_ref,
    th_ref,
    s_in,
    flat,
    flat2,
    side_flat,
    side,
    side_buf,
    stage,
    rbuf,
    seen,
    seen_buf,
    stage2,
    rbuf2,
    d_mine,
    d_other,
    m_s,
    mt_s,
    th_s,
    plane_s,
    pst,
    g_s,
    tail_s,
    tail_r,
    s_side,
    r_side,
    s_pay,
    r_pay,
    s_seen,
    r_seen,
    s_del,
    r_del,
    s_tail,
    r_tail,
    s_out,
    r_out,
):
    n, width, channels, taps, chunks, rows, depth = dims
    v = lax.axis_index("vessel")
    me = lax.axis_index("gather")
    other = 1 - v
    nt = width // LANES
    group = rows // n
    f32, bf16 = jnp.float32, jnp.bfloat16

    loads = [
        pltpu.make_async_copy(source, target, s_in.at[i])
        for i, (source, target) in enumerate(
            (
                (x_hbm.at[0, 0], x_ref),
                (obs_hbm.at[0], obs_ref),
                (tt_hbm, tt_ref),
                (ts_hbm, ts_ref),
                (th_hbm, th_ref),
            )
        )
    ]
    for load in loads[:2]:
        load.start()

    barrier = pltpu.get_barrier_semaphore()

    def greet(i, carry):
        p = partner_of(me, i, n)
        pl.semaphore_signal(barrier, inc=1, device_id=(v, p), device_id_type=MESH)
        pl.semaphore_signal(barrier, inc=1, device_id=(other, p), device_id_type=MESH)
        return carry

    lax.fori_loop(1, n, greet, 0)
    pl.semaphore_signal(barrier, inc=1, device_id=(other, me), device_id_type=MESH)
    for load in loads[2:]:
        load.start()

    side_flat[...] = jnp.zeros((n * SIDE, LANES), f32)
    plane_s[:, :LANES] = jnp.zeros((n, LANES), bf16)
    plane_s[:, LANES + width :] = jnp.zeros((n, LANES), bf16)
    if depth > taps * n:
        pst[taps * n :, :] = jnp.zeros((depth - taps * n, width), bf16)

    def put(ref, i, stride, value):
        ref[pl.ds(i, n, stride=stride), :] = value

    def take(ref, i, stride):
        return ref[pl.ds(i, n, stride=stride), :]

    def tiles_of(ref):
        return [ref[:, i * LANES : (i + 1) * LANES].astype(f32) for i in range(nt)]

    for load in loads[:2]:
        load.wait()
    d = jnp.full((n, LANES), d_hbm[0, 0], jnp.int32)
    lane = lane_of((n, LANES))
    most = MAXD // LANES

    put(side_flat, 0, SIDE, d.astype(f32))
    tiles = tiles_of(x_ref)
    for j in range(most):
        put(side_flat, 2 + j, SIDE, tiles[nt - most + j])
    side[...] = side_flat[...].reshape(n, SIDE, LANES).astype(bf16)
    moved = shift_rows([None] * most + tiles, MAXD - d, nt, most)
    tiles = tiles_of(obs_ref)
    for i in range(nt):
        put(flat, i, nt, tiles[i] - moved[i])
    stage[...] = flat[...].reshape(n, nt, LANES).astype(bf16)

    pl.semaphore_wait(barrier, 2 * n - 1)

    def hand(src, dst, send_sem, recv_sem, vessel, p):
        return pltpu.make_async_remote_copy(
            src_ref=src,
            dst_ref=dst,
            send_sem=send_sem,
            recv_sem=recv_sem,
            device_id=(vessel, p),
            device_id_type=MESH,
        )

    def batch(src, dst, send_sem, recv_sem, vessel, count):
        def one(p):
            return hand(src.at[p], dst.at[me], send_sem, recv_sem, vessel, p)

        return one, hand(src.at[pl.ds(0, count)], dst.at[pl.ds(0, count)], send_sem, recv_sem, vessel, me)

    cross, all_cross = batch(side, side_buf, s_side, r_side, other, n)
    payload, all_payload = batch(stage, rbuf, s_pay, r_pay, v, n - 1)
    later, all_later = batch(seen, seen_buf, s_seen, r_seen, v, n - 1)
    result, all_result = batch(stage2, rbuf2, s_out, r_out, v, n - 1)

    def to_all(copy):
        def send(i, carry):
            copy(partner_of(me, i, n)).start()
            return carry

        lax.fori_loop(1, n, send, 0)

    to_all(cross)
    to_all(payload)
    cross(me).start()
    rbuf[me] = stage[me]

    moved = shift_rows(tiles_of(obs_ref), d, nt, most)
    for i in range(nt):
        put(flat2, i, nt, moved[i])
    seen[...] = flat2[...].reshape(n, nt, LANES).astype(bf16)
    to_all(later)
    seen_buf[me] = seen[me]

    for load in loads[2:]:
        load.wait()

    def build(q, carry):
        row_ch = q * group + lax.broadcasted_iota(jnp.int32, (rows, channels), 0) // n
        pick = row_ch == lax.broadcasted_iota(jnp.int32, (rows, channels), 1)
        pick_f = pick.astype(f32)
        tt = lax.dot_general(pick_f, tt_ref[...], (((1,), (1,)), ((), ())), precision=lax.Precision.HIGHEST, preferred_element_type=f32)
        ts = lax.dot_general(pick_f, ts_ref[...], (((1,), (1,)), ((), ())), precision=lax.Precision.HIGHEST, preferred_element_type=f32)
        th_s[q] = jnp.broadcast_to(jnp.sum(jnp.where(pick, th_ref[...], 0.0), axis=1, keepdims=True), (rows, LANES))
        col = lax.broadcasted_iota(jnp.int32, (rows, depth), 1)
        row = lax.broadcasted_iota(jnp.int32, (rows, depth), 0)
        apart = lax.rem(col, n) - lax.rem(row, n)
        tap_of = col // n
        a = jnp.zeros((rows, depth), f32)
        b = jnp.zeros((rows, depth), f32)
        for k in range(taps):
            a = jnp.where(tap_of == k, tt[:, k : k + 1], a)
            b = jnp.where(apart == (k - REACH) * SHOT_SPACING, ts[:, k : k + 1], b)
        m = a * b
        m_s[q] = m.astype(bf16)
        mt_s[q] = m.T.astype(bf16)
        return carry

    if chunks == 1:
        build(0, 0)
    else:
        lax.fori_loop(0, chunks, build, 0)

    block_width = 2048

    def filter_columns(start, stop):
        def one(q, first):
            for c0 in range(start, stop, block_width):
                c1 = min(c0 + block_width, stop)
                y = jnp.dot(m_s[q], pst[:, c0:c1], preferred_element_type=f32)
                th = across(th_s[q], c1 - c0)
                z = (y - jnp.minimum(jnp.maximum(y, -th), th)).astype(bf16)
                g = jnp.dot(mt_s[q], z, preferred_element_type=f32)
                if first:
                    g_s[:, c0:c1] = g
                else:
                    g_s[:, c0:c1] += g

        one(0, True)
        if chunks > 1:

            def more(q, carry):
                one(q, False)
                return carry

            lax.fori_loop(1, chunks, more, 0)

    def stack_taps(start, stop):
        lo = start
        piece = plane_s[:, lo : stop + 2 * LANES]
        extent = piece.shape[1]
        for k in range(taps):
            step = (k - REACH) * TIME_SPACING
            moved = piece if step == 0 else pltpu.roll(piece, (extent - step) % extent, 1)
            pst[k * n : (k + 1) * n, start:stop] = moved[:, LANES : LANES + stop - start]

    def collect():
        total = jnp.zeros((n, width), f32)
        for k in range(taps):
            step = (k - REACH) * TIME_SPACING
            g = g_s[k * n : (k + 1) * n, :]
            if step != 0:
                extent = width + LANES
                g = pltpu.roll(jnp.concatenate([g, jnp.zeros((n, LANES), f32)], axis=1), step % extent, 1)[:, :width]
            total = total + g
        return total.astype(bf16)

    def store_plane(i, value):
        plane_s[:, LANES + i * LANES : LANES + (i + 1) * LANES] = value.astype(bf16)

    cut = nt - most

    def before_end(i, delay):
        return i * LANES + lane + delay < width

    all_cross.wait_recv()
    side_flat[...] = side_buf[...].astype(f32).reshape(n * SIDE, LANES)
    theirs = take(side_flat, 0, SIDE).astype(jnp.int32)
    d_other[...] = theirs
    swap = hand(d_other, d_mine, s_del, r_del, other, me)
    swap.start()

    all_payload.wait_recv()
    flat[...] = rbuf[...].astype(f32).reshape(n * nt, LANES)
    moved = shift_rows([take(flat, i, nt) for i in range(nt)], theirs, nt, most)
    for i in range(nt):
        value = moved[i]
        if i >= cut:
            value = jnp.where(before_end(i, theirs), value, take(side_flat, 2 + i - cut, SIDE))
        store_plane(i, value)
    stack_taps(0, width)
    filter_columns(0, width)
    held = collect()
    tail_s[...] = held[:, width - MAXD :]
    trade = hand(tail_s, tail_r, s_tail, r_tail, other, me)
    trade.start()
    all_later.wait_recv()
    swap.wait_recv()
    flat2[...] = seen_buf[...].astype(f32).reshape(n * nt, LANES)
    ours = d_mine[...]
    tiles = [None] * most + [held[:, i * LANES : (i + 1) * LANES].astype(f32) for i in range(nt)]
    moved = shift_rows(tiles, ours - theirs + MAXD, nt, 2 * most)
    for i in range(cut):
        store_plane(i, take(flat2, i, nt) - moved[i])
    trade.wait_recv()
    for i in range(cut, nt):
        end = tail_r[:, (i - cut) * LANES : (i - cut + 1) * LANES].astype(f32)
        store_plane(i, jnp.where(before_end(i, ours), take(flat2, i, nt) - moved[i], end))
    stack_taps(0, width)
    filter_columns(0, width)
    held = collect()

    for i in range(nt):
        put(flat, i, nt, held[:, i * LANES : (i + 1) * LANES].astype(f32))
    stage2[...] = flat[...].reshape(n, nt, LANES).astype(bf16)
    to_all(result)
    rbuf2[me] = stage2[me]

    all_cross.wait_send()
    all_payload.wait_send()
    all_later.wait_send()
    swap.wait_send()
    trade.wait_send()

    all_result.wait_recv()
    flat[...] = rbuf2[...].astype(f32).reshape(n * nt, LANES)
    for i in range(nt):
        out_ref[0, 0, :, i * LANES : (i + 1) * LANES] = take(flat, i, nt).astype(bf16)
    all_result.wait_send()


def per_device(n, observed, estimate, delays, taps_time, taps_shot, thresh):
    receivers, width = observed.shape[1:]
    channels, taps = taps_time.shape
    assert observed.shape[0] == 1 and receivers == n and width % LANES == 0
    group = max(1, min(channels, 256 // n))
    chunks = channels // group
    rows = group * n
    depth = -(-taps * n // LANES) * LANES
    nt = width // LANES
    bf16, f32 = jnp.bfloat16, jnp.float32
    vmem = pl.BlockSpec(memory_space=pltpu.VMEM)
    dma = pltpu.SemaphoreType.DMA
    operands = (estimate, observed, delays, taps_time.T, taps_shot.T, thresh.reshape(1, channels))
    operands = [o if o is delays else pltpu.with_memory_space_constraint(o, pltpu.HBM) for o in operands]
    return pl.pallas_call(
        functools.partial(kernel, (n, width, channels, taps, chunks, rows, depth)),
        out_shape=pltpu.VMEM(estimate.shape, bf16),
        in_specs=[pl.BlockSpec(memory_space=pltpu.SMEM if i == 2 else pl.ANY) for i in range(6)],
        out_specs=vmem,
        scratch_shapes=[
            pltpu.VMEM((n, width), bf16),
            pltpu.VMEM((n, width), bf16),
            pltpu.VMEM((taps, channels), f32),
            pltpu.VMEM((taps, channels), f32),
            pltpu.VMEM((1, channels), f32),
            dma((5,)),
            pltpu.VMEM((n * nt, LANES), f32),
            pltpu.VMEM((n * nt, LANES), f32),
            pltpu.VMEM((n * SIDE, LANES), f32),
            pltpu.VMEM((n, SIDE, LANES), bf16),
            pltpu.VMEM((n, SIDE, LANES), bf16),
            pltpu.VMEM((n, nt, LANES), bf16),
            pltpu.VMEM((n, nt, LANES), bf16),
            pltpu.VMEM((n, nt, LANES), bf16),
            pltpu.VMEM((n, nt, LANES), bf16),
            pltpu.VMEM((n, nt, LANES), bf16),
            pltpu.VMEM((n, nt, LANES), bf16),
            pltpu.VMEM((n, LANES), jnp.int32),
            pltpu.VMEM((n, LANES), jnp.int32),
            pltpu.VMEM((chunks, rows, depth), bf16),
            pltpu.VMEM((chunks, depth, rows), bf16),
            pltpu.VMEM((chunks, rows, LANES), f32),
            pltpu.VMEM((n, width + 2 * LANES), bf16),
            pltpu.VMEM((depth, width), bf16),
            pltpu.VMEM((depth, width), f32),
            pltpu.VMEM((n, MAXD), bf16),
            pltpu.VMEM((n, MAXD), bf16),
        ]
        + [dma(())] * 12,
        compiler_params=pltpu.CompilerParams(collective_id=0, has_side_effects=True, vmem_limit_bytes=48 << 20),
    )(*operands)


def solution(mesh):
    return jax.shard_map(
        functools.partial(per_device, mesh.shape["gather"]),
        mesh=mesh,
        in_specs=(
            P("gather", None, None),
            P("vessel", "gather", None, None),
            P("vessel", "gather"),
            P(),
            P(),
            P(),
        ),
        out_specs=P("vessel", "gather", None, None),
        check_vma=False,
    )
```

time: 24.5 us -> 20.6 us (0.84)
  Pallas kernels: 23.1 us -> 19.2 us
    pallas_call x1, Pallas kernels: 23.1 us -> 19.2 us  [per_device(): pl.pallas_call(functools.partial(kernel, (n, width, channels, taps, chunk...]
where the time goes in v1:
time: 20.6 us; the launch traced here: 20.5 us
  Pallas kernels  19.2 us (93%)
  between operations  0.66 us (3%)
  local copies, waits for them, and re-layouts  0.63 us (3%)
    pallas_call x1, Pallas kernels, per_device(): pl.pallas_call(functools.partial(kernel, (n, width, channels, taps, chunk...  19.2 us
    unnamed x1, local copies, waits for them, and re-layouts  0.63 us

profile of v1, /device:TPU:0, one launch (start us, length us, event | category | flops | bytes accessed | tf_op | source)
XLA Modules:
  0.0 20.5 jit_solution(11752273280510717104)
XLA Ops:
  0.7 19.2 %shard_map.64 = bf16[1,1,16,2048]{3,2,1,0:T(8,128)(2,1)S(1)} custom-call(bf16[1,1,16,2048]{3,2,1,0:T(8,128)(2,1)} %x_hbm.1, bf16[1,16,2048]{2,1,0:T(8,128)(2,1)} %obs_hbm.1, s32[1,1]{1,0:T(1,128)S(6)} %copy.9.d_hbm, f32[7,16]{1,0:T(8,128)} %bitcast.3, f32[7,16]{1,0:T(8,128)} %bitcast.4, f32[1,16]{1,0:T(1,128)} %bitcast.5), custom_call_target="tpu_custom_call" | custom-call | tf_op jit(solution)/shard_map/pallas_call | solution.py:371
  19.8 0.6 %copy.8 = bf16[1,1,16,2048]{3,2,1,0:T(8,128)(2,1)} copy(bf16[1,1,16,2048]{3,2,1,0:T(8,128)(2,1)S(1)} %shard_map.64) | data formatting | bytes 131072
